TPU v7x, 256 devices: a whole 4x4x8 slice. The times are simulated.
256 devices in a mesh: src: 32 (over y, z), dst: 8 (over x, core).
Axes of the slice: x: 4, y: 4, z: 8, core: 2. Of those that a mesh axis runs over, the one named last changes fastest.
Arguments:
- transition: bfloat16 [16384, 16384], P('src', 'dst'), may hold values from 5.4931641e-06 to 0.05
- emission: bfloat16 [8192, 16384], P('src', 'dst'), may hold values from 0.099609375 to 5
- forward: bfloat16 [3, 256, 16384], P(None, None, 'src'), may hold values from 0.25 to 4
- beta_end: bfloat16 [256, 16384], P(None, 'dst'), may hold values from 0.5 to 2
- scales: float32 [3, 256], replicated, may hold values from 0.5 to 2
- tokens: int32 [3, 256], replicated, may hold values from 0 to 8191
Outputs:
- counts: float32 [16384, 16384], P('src', 'dst')
- beta_first: float32 [256, 16384], P('dst', 'src')
All inputs are finite; a program needn't handle non-finite values.
Results may differ from a plain program's by a relative error of at most 0.00076.
Values may be sent and summed in bfloat16 or wider, within the bound.
A program may use at most 64 MiB of HBM per device.

v0:
```python
import jax
import jax.numpy as jnp
from jax import lax
from jax.sharding import PartitionSpec as P

B = 256
STEPS = 3


def local_rows(words, emission, first_word):
    keys = words - first_word
    table = (keys[:, None] == jnp.arange(emission.shape[0], dtype=jnp.int32)[None, :]).astype(
        jnp.bfloat16
    )
    return jnp.dot(table, emission, preferred_element_type=jnp.bfloat16)


def emitted_window(words, emission, first_word):
    return (
        lax.psum(local_rows(words, emission, first_word), "src")
        .astype(jnp.float32)
        .astype(jnp.bfloat16)
    )


def per_device(transition, emission, forward, beta_end, scales, tokens):
    steps = forward.shape[0]
    batch = forward.shape[1]
    src_cols = transition.shape[0]
    dst_cols = transition.shape[1]
    n_dst = lax.axis_size("dst")
    share = batch // n_dst
    first_word = lax.axis_index("src") * emission.shape[0]
    emitted_all = emitted_window(tokens.reshape(-1), emission, first_word).reshape(
        steps, batch, dst_cols
    )
    message = beta_end
    pairs = jnp.zeros((src_cols, dst_cols), jnp.float32)
    beta_first = jnp.zeros((share, src_cols), jnp.float32)
    for step in range(steps - 1, -1, -1):
        emitted = emitted_all[step]
        weighted = (
            emitted.astype(jnp.float32) * message.astype(jnp.float32) / scales[step][:, None]
        ).astype(jnp.bfloat16)
        pairs = pairs + lax.dot_general(
            forward[step], weighted, (((0,), (0,)), ((), ())), preferred_element_type=jnp.float32
        )
        partial_rows = lax.dot_general(
            weighted, transition, (((1,), (1,)), ((), ())), preferred_element_type=jnp.float32
        )
        summed = lax.psum(partial_rows, "dst")
        if step == 0:
            beta_first = lax.dynamic_slice_in_dim(summed, lax.axis_index("dst") * share, share, 0)
        else:
            gathered = lax.all_gather(summed.astype(jnp.bfloat16), "src", axis=1, tiled=True)
            message = lax.dynamic_slice_in_dim(
                gathered, lax.axis_index("dst") * dst_cols, dst_cols, 1
            )
    counts = transition.astype(jnp.float32) * pairs * (32.0 / (STEPS * B))
    return (counts, beta_first)


def solution(mesh):
    in_specs = (P("src", "dst"), P("src", "dst"), P(None, None, "src"), P(None, "dst"), P(), P())
    out_specs = (P("src", "dst"), P("dst", "src"))
    return jax.shard_map(
        per_device, mesh=mesh, in_specs=in_specs, out_specs=out_specs, check_vma=False
    )
```

profile of v0, /device:TPU:8, one launch (start us, length us, event | category | flops | bytes accessed | tf_op | source)
XLA Modules:
  0.0 517.3 jit_solution(17679597140141207824)
XLA Ops:
  7.2 0.8 broadcast_subtract_fusion
  8.4 2.7 fusion.1
  11.2 0.6 copy-done.7
  11.8 160.7 %all-reduce.5.cloned.1.call-done = bf16[768,2048]{1,0:T(8,128)(2,1)} async-done(((bf16[768,2048]{1,0:T(8,128)(2,1)}), bf16[768,2048]{1,0:T(8,128)(2,1)}) %all-reduce.5.cloned.1.call-update) | async-done | bytes 3145744 | tf_op jit(solution)/shard_map/psum | solution.py:20
  172.5 2.0 divide_convert_fusion.2
  174.4 1.0 copy-done.1
  175.5 1.5 fusion.12
  177.0 30.2 %all-reduce.8 = bf16[256,512]{1,0:T(8,128)(2,1)} all-reduce(f32[256,512]{1,0:T(8,128)} %fusion.12), channel_id=1, replica_groups=mesh['src'=32,'dst'=8] {'dst'}, use_global_device_ids=true, to_apply=%region_1.0 | all-reduce | flops 131072 | bytes 786432 | tf_op jit(solution)/shard_map/psum | solution.py:51
  207.3 98.0 %all-gather.3.cloned.1.call-done = bf16[256,16384]{1,0:T(8,128)(2,1)} async-done(((bf16[256,512]{1,0:T(8,128)(2,1)}), bf16[256,16384]{1,0:T(8,128)(2,1)}) %all-gather.3.cloned.1.call-update) | async-done | bytes 8388624 | tf_op jit(solution)/shard_map/all_gather | solution.py:55
  305.3 2.0 divide_convert_fusion.1
  307.2 0.9 copy-done.2
  308.2 1.5 fusion.13
  309.7 30.2 %all-reduce.9 = bf16[256,512]{1,0:T(8,128)(2,1)} all-reduce(f32[256,512]{1,0:T(8,128)} %fusion.13), channel_id=1, replica_groups=mesh['src'=32,'dst'=8] {'dst'}, use_global_device_ids=true, to_apply=%region_2.0 | all-reduce | flops 131072 | bytes 786432 | tf_op jit(solution)/shard_map/psum | solution.py:51
  340.0 2.9 copy.8
  342.9 4.1 fusion.6
  347.0 3.7 fusion.4
  350.6 88.1 %all-gather.5.cloned.1.call-done = bf16[256,16384]{1,0:T(8,128)(2,1)} async-done(((bf16[256,512]{1,0:T(8,128)(2,1)}), bf16[256,16384]{1,0:T(8,128)(2,1)}) %all-gather.5.cloned.1.call-update) | async-done | bytes 8388624 | tf_op jit(solution)/shard_map/all_gather | solution.py:55
  438.8 2.1 divide_convert_fusion
  440.9 1.0 copy-done.4
  441.9 1.5 fusion.14
  443.4 6.9 %fusion = f32[512,2048]{0,1:T(8,128)} fusion(f32[2048,512]{1,0:T(8,128)} %fusion.6, f32[2048,512]{1,0:T(8,128)} %fusion.4, bf16[512,2048]{0,1:T(8,128)(2,1)S(1)} %copy.8, bf16[256,2048]{1,0:T(8,128)(2,1)} %copy-done.4, bf16[3,256,512]{2,1,0:T(8,128)(2,1)} %param.8), kind=kOutput, calls=%fused_computation.1 | convolution fusion | flops 542113792 | bytes 15990784 | tf_op jit(solution)/shard_map/dot_general | solution.py:45
  450.3 5.3 %copy.9 = f32[512,2048]{1,0:T(8,128)} copy(f32[512,2048]{0,1:T(8,128)} %fusion) | data formatting | bytes 8388608
  455.7 53.7 %all-reduce.7.cloned.1.call-done = f32[256,512]{1,0:T(8,128)} async-done(((f32[256,512]{1,0:T(8,128)}), f32[256,512]{1,0:T(8,128)}) %all-reduce.7.cloned.1.call-update) | async-done | bytes 524304 | tf_op jit(solution)/shard_map/psum | solution.py:51
  509.3 1.5 constant_dynamic-slice_fusion
  (22 shorter events, 0.7 us)
Async XLA Ops:
  7.2 1.2 copy-start
  7.2 165.3 %all-reduce.5.cloned.1.call-start = ((), (), s32[]{:S(2)}) async-start(), calls=%async_computation | async-start | bytes 6291456 | tf_op jit(solution)/shard_map/psum | solution.py:20
  11.1 0.7 copy-start.7
  11.1 164.4 %copy-start.5 = (bf16[512,2048]{1,0:T(8,128)(2,1)S(1)}, bf16[512,2048]{1,0:T(8,128)(2,1)}, u32[]{:S(2)}) copy-start(bf16[512,2048]{1,0:T(8,128)(2,1)} %param.6) | copy-start | bytes 6291460
  11.1 294.1 %all-gather.3.cloned.1.call-start = ((), (), s32[]{:S(2)}) async-start(), calls=%async_computation.1 | async-start | bytes 8650752 | tf_op jit(solution)/shard_map/all_gather | solution.py:55
  174.4 1.1 copy-start.1
  207.2 231.5 %all-gather.5.cloned.1.call-start = ((), (), s32[]{:S(2)}) async-start(), calls=%async_computation.2 | async-start | bytes 8650752 | tf_op jit(solution)/shard_map/all_gather | solution.py:55
  307.2 1.0 copy-start.2
  339.9 169.4 %all-reduce.7.cloned.1.call-start = ((), (), s32[]{:S(2)}) async-start(), calls=%async_computation.3 | async-start | bytes 1048576 | tf_op jit(solution)/shard_map/psum | solution.py:51
  342.8 4.1 copy-start.3
  438.8 3.1 copy-start.6
  440.9 1.0 copy-start.4
Sparse Core Ops, SparseCore 0:
  12.1 160.3 all-reduce.4
  207.4 97.8 all-gather.2
  340.0 98.6 all-gather.4
  443.5 65.7 all-reduce.6
where the time goes:
time: 518 us; the launch traced here: 517 us
  waiting for transfers between devices  400 us (77%)
  blocking collectives  60.3 us (12%)
  matrix products  22 us (4%)
  between operations  13.9 us (3%)
  local copies, waits for them, and re-layouts  13.7 us (3%)
  other arithmetic  6.79 us (1%)
    all_gather x2, waiting for transfers between devices, per_device(): lax.all_gather(summed.astype(jnp.bfloat16), 'src', axis=1, tiled=True)  186 us
    psum x1, waiting for transfers between devices, emitted_window(): lax.psum(local_rows(words, emission, first_word), 'src').astype(jnp.float32)  161 us
    psum x2, blocking collectives, per_device(): summed = lax.psum(partial_rows, 'dst')  60.3 us
    psum x1, waiting for transfers between devices, per_device(): summed = lax.psum(partial_rows, 'dst')  53.7 us
    dot_general x3, matrix products, per_device(): lax.dot_general(forward[step], weighted, (((0,), (0,)), ((), ())), prefer...  14.7 us
    unnamed x18, local copies, waits for them, and re-layouts  12.2 us
  transfers between devices with their start and end apart: 4, of which 4 were waited for; matrix products, arithmetic and copies ran while one was open for 4% of the time, Pallas kernels for 0%

commit v1 on v0

--- a/solution.py
+++ b/solution.py
@@ -48,7 +48,9 @@
         partial_rows = lax.dot_general(
             weighted, transition, (((1,), (1,)), ((), ())), preferred_element_type=jnp.float32
         )
-        summed = lax.psum(partial_rows, "dst")
+        summed = partial_rows
+        for hop in (1, 2, 4):
+            summed = summed + lax.ppermute(summed, "dst", [(dev, dev ^ hop) for dev in range(8)])
         if step == 0:
             beta_first = lax.dynamic_slice_in_dim(summed, lax.axis_index("dst") * share, share, 0)
         else:

time: 518 us -> 492 us (0.950)
  blocking collectives: 60.3 us -> 0 us
  waiting for transfers between devices: 400 us -> 429 us
  starting transfers between devices: 0.16 us -> 14.1 us
  matrix products: 22 us -> 11.2 us
  other arithmetic: 6.79 us -> 12.3 us
    ppermute x0 -> x9, waiting for transfers between devices: none -> 66.4 us  [per_device(): lax.ppermute(summed, 'dst', [(dev, dev ^ hop) for dev in range(8)])]
    psum x2 -> x0, blocking collectives: 60.3 us -> none  [per_device(): summed = lax.psum(partial_rows, 'dst')]
    psum x1 -> x0, waiting for transfers between devices: 53.7 us -> none  [per_device(): summed = lax.psum(partial_rows, 'dst')]
    all_gather x2, waiting for transfers between devices: 186 us -> 202 us  [per_device(): lax.all_gather(summed.astype(jnp.bfloat16), 'src', axis=1, tiled=True)]
    ppermute x0 -> x9, starting transfers between devices: none -> 14 us  [per_device(): lax.ppermute(summed, 'dst', [(dev, dev ^ hop) for dev in range(8)])]
    dot_general x3, matrix products: 14.7 us -> 5.44 us  [per_device(): lax.dot_general(forward[step], weighted, (((0,), (0,)), ((), ())), prefer...]
    unnamed x18 -> x22, local copies, waits for them, and re-layouts: 12.2 us -> 10.3 us
  transfers between devices with their start and end apart: 4 -> 12, of which waited for: 4 -> 11; matrix products, arithmetic and copies ran while one was open for 4% -> 3% of each run, Pallas kernels for 0% -> 0%
where the time goes in v1:
time: 492 us; the launch traced here: 491 us
  waiting for transfers between devices  429 us (87%)
  starting transfers between devices  14.1 us (3%)
  between operations  14 us (3%)
  other arithmetic  12.3 us (2%)
  matrix products  11.2 us (2%)
  local copies, waits for them, and re-layouts  10.3 us (2%)
    all_gather x2, waiting for transfers between devices, per_device(): lax.all_gather(summed.astype(jnp.bfloat16), 'src', axis=1, tiled=True)  202 us
    psum x1, waiting for transfers between devices, emitted_window(): lax.psum(local_rows(words, emission, first_word), 'src').astype(jnp.float32)  161 us
    ppermute x9, waiting for transfers between devices, per_device(): lax.ppermute(summed, 'dst', [(dev, dev ^ hop) for dev in range(8)])  66.4 us
    ppermute x9, starting transfers between devices, per_device(): lax.ppermute(summed, 'dst', [(dev, dev ^ hop) for dev in range(8)])  14 us
    unnamed x22, local copies, waits for them, and re-layouts  10.3 us
  transfers between devices with their start and end apart: 12, of which 11 were waited for; matrix products, arithmetic and copies ran while one was open for 3% of the time, Pallas kernels for 0%

profile of v1, /device:TPU:8, one launch (start us, length us, event | category | flops | bytes accessed | tf_op | source)
XLA Modules:
  0.0 490.5 jit_solution(15180645733023756691)
XLA Ops:
  8.4 2.7 fusion.1
  11.8 160.7 %all-reduce.2.cloned.1.call-done = bf16[768,2048]{1,0:T(8,128)(2,1)} async-done(((bf16[768,2048]{1,0:T(8,128)(2,1)}), bf16[768,2048]{1,0:T(8,128)(2,1)}) %all-reduce.2.cloned.1.call-update) | async-done | bytes 3145744 | tf_op jit(solution)/shard_map/psum | solution.py:20
  172.5 2.0 divide_convert_fusion.2
  175.3 1.9 collective-permute-done
  178.8 12.5 %collective-permute-done.1 = f32[256,512]{1,0:T(8,128)S(1)} collective-permute-done((f32[256,512]{1,0:T(8,128)S(1)}, f32[256,512]{1,0:T(8,128)S(1)}, u32[]{:S(2)}, u32[]{:S(2)}) %collective-permute-start.1) | collective-permute-done | bytes 524320 | tf_op jit(solution)/shard_map/ppermute | solution.py:53
  191.4 3.1 collective-permute-start.2
  194.5 11.6 %collective-permute-done.2 = f32[256,512]{1,0:T(8,128)S(1)} collective-permute-done((f32[256,512]{1,0:T(8,128)S(1)}, f32[256,512]{1,0:T(8,128)S(1)}, u32[]{:S(2)}, u32[]{:S(2)}) %collective-permute-start.2) | collective-permute-done | bytes 524320 | tf_op jit(solution)/shard_map/ppermute | solution.py:53
  207.0 100.3 %all-gather.3.cloned.1.call-done = bf16[256,16384]{1,0:T(8,128)(2,1)} async-done(((bf16[256,512]{1,0:T(8,128)(2,1)}), bf16[256,16384]{1,0:T(8,128)(2,1)}) %all-gather.3.cloned.1.call-update) | async-done | bytes 8388624 | tf_op jit(solution)/shard_map/all_gather | solution.py:57
  307.3 2.0 divide_convert_fusion.1
  310.1 1.9 collective-permute-done.3
  312.1 1.6 collective-permute-start.4
  313.7 12.5 %collective-permute-done.4 = f32[256,512]{1,0:T(8,128)S(1)} collective-permute-done((f32[256,512]{1,0:T(8,128)S(1)}, f32[256,512]{1,0:T(8,128)S(1)}, u32[]{:S(2)}, u32[]{:S(2)}) %collective-permute-start.4) | collective-permute-done | bytes 524320 | tf_op jit(solution)/shard_map/ppermute | solution.py:53
  326.3 3.1 collective-permute-start.5
  329.3 11.6 %collective-permute-done.5 = f32[256,512]{1,0:T(8,128)S(1)} collective-permute-done((f32[256,512]{1,0:T(8,128)S(1)}, f32[256,512]{1,0:T(8,128)S(1)}, u32[]{:S(2)}, u32[]{:S(2)}) %collective-permute-start.5) | collective-permute-done | bytes 524320 | tf_op jit(solution)/shard_map/ppermute | solution.py:53
  341.8 101.2 %all-gather.5.cloned.1.call-done = bf16[256,16384]{1,0:T(8,128)(2,1)} async-done(((bf16[256,512]{1,0:T(8,128)(2,1)}), bf16[256,16384]{1,0:T(8,128)(2,1)}) %all-gather.5.cloned.1.call-update) | async-done | bytes 8388624 | tf_op jit(solution)/shard_map/all_gather | solution.py:57
  443.0 2.0 divide_convert_fusion
  446.0 1.6 fusion.14
  447.6 2.9 copy.8
  453.4 1.7 fusion.6
  455.9 10.4 %collective-permute-done.7 = f32[256,512]{1,0:T(8,128)S(1)} collective-permute-done((f32[256,512]{1,0:T(8,128)S(1)}, f32[256,512]{1,0:T(8,128)S(1)}, u32[]{:S(2)}, u32[]{:S(2)}) %collective-permute-start.7) | collective-permute-done | bytes 524320 | tf_op jit(solution)/shard_map/ppermute | solution.py:53
  467.2 3.0 collective-permute-start.8
  470.2 3.0 fusion
  473.2 5.3 %copy.9 = f32[512,2048]{1,0:T(8,128)} copy(f32[512,2048]{0,1:T(8,128)} %fusion) | data formatting | bytes 8388608
  478.5 4.0 collective-permute-done.8
  (47 shorter events, 14.2 us)
Async XLA Ops:
  7.2 1.2 copy-start
  7.2 165.3 %all-reduce.2.cloned.1.call-start = ((), (), s32[]{:S(2)}) async-start(), calls=%async_computation | async-start | bytes 6291456 | tf_op jit(solution)/shard_map/psum | solution.py:20
  11.1 0.7 copy-start.9
  11.1 163.3 %copy-start.7 = (bf16[512,2048]{1,0:T(8,128)(2,1)S(1)}, bf16[512,2048]{1,0:T(8,128)(2,1)}, u32[]{:S(2)}) copy-start(bf16[512,2048]{1,0:T(8,128)(2,1)} %param.6) | copy-start | bytes 6291460
  11.1 296.2 %all-gather.3.cloned.1.call-start = ((), (), s32[]{:S(2)}) async-start(), calls=%async_computation.1 | async-start | bytes 8650752 | tf_op jit(solution)/shard_map/all_gather | solution.py:57
  174.4 2.8 copy-start.1
  175.2 2.0 collective-permute-start
  177.3 14.1 %collective-permute-start.1 = (f32[256,512]{1,0:T(8,128)S(1)}, f32[256,512]{1,0:T(8,128)S(1)}, u32[]{:S(2)}, u32[]{:S(2)}) collective-permute-start(f32[256,512]{1,0:T(8,128)S(1)} %add.46), channel_id=1, source_target_pairs={{0,2},{1,3},{2,0},{3,1},{4,6},{5,7},{6,4},{7,5},{8,10},{9,11},{10,... | collective-permute-start | bytes 1572872 | tf_op jit(solution)/shard_map/ppermute | solution.py:53
  191.4 14.7 %collective-permute-start.2 = (f32[256,512]{1,0:T(8,128)S(1)}, f32[256,512]{1,0:T(8,128)S(1)}, u32[]{:S(2)}, u32[]{:S(2)}) collective-permute-start(f32[256,512]{1,0:T(8,128)S(1)} %add.47), channel_id=1, source_target_pairs={{0,4},{1,5},{2,6},{3,7},{4,0},{5,1},{6,2},{7,3},{8,12},{9,13},{10,... | collective-permute-start | bytes 1572872 | tf_op jit(solution)/shard_map/ppermute | solution.py:53
  206.9 236.1 %all-gather.5.cloned.1.call-start = ((), (), s32[]{:S(2)}) async-start(), calls=%async_computation.2 | async-start | bytes 8650752 | tf_op jit(solution)/shard_map/all_gather | solution.py:57
  309.3 2.9 copy-start.3
  310.0 2.0 collective-permute-start.3
  312.1 14.1 %collective-permute-start.4 = (f32[256,512]{1,0:T(8,128)S(1)}, f32[256,512]{1,0:T(8,128)S(1)}, u32[]{:S(2)}, u32[]{:S(2)}) collective-permute-start(f32[256,512]{1,0:T(8,128)S(1)} %add.51), channel_id=1, source_target_pairs={{0,2},{1,3},{2,0},{3,1},{4,6},{5,7},{6,4},{7,5},{8,10},{9,11},{10,... | collective-permute-start | bytes 1572872 | tf_op jit(solution)/shard_map/ppermute | solution.py:53
  326.3 14.7 %collective-permute-start.5 = (f32[256,512]{1,0:T(8,128)S(1)}, f32[256,512]{1,0:T(8,128)S(1)}, u32[]{:S(2)}, u32[]{:S(2)}) collective-permute-start(f32[256,512]{1,0:T(8,128)S(1)} %add.52), channel_id=1, source_target_pairs={{0,4},{1,5},{2,6},{3,7},{4,0},{5,1},{6,2},{7,3},{8,12},{9,13},{10,... | collective-permute-start | bytes 1572872 | tf_op jit(solution)/shard_map/ppermute | solution.py:53
  445.0 1.0 copy-start.5
  447.6 2.9 collective-permute-start.6
  450.4 3.0 copy-start.2
  451.8 3.3 copy-start.4
  451.8 3.3 copy-start.8
  451.9 14.4 %collective-permute-start.7 = (f32[256,512]{1,0:T(8,128)S(1)}, f32[256,512]{1,0:T(8,128)S(1)}, u32[]{:S(2)}, u32[]{:S(2)}) collective-permute-start(f32[256,512]{1,0:T(8,128)S(1)} %add.56), channel_id=1, source_target_pairs={{0,2},{1,3},{2,0},{3,1},{4,6},{5,7},{6,4},{7,5},{8,10},{9,11},{10,... | collective-permute-start | bytes 1572872 | tf_op jit(solution)/shard_map/ppermute | solution.py:53
  455.9 14.3 %copy-start.6 = (bf16[256,2048]{1,0:T(8,128)(2,1)S(1)}, bf16[256,2048]{1,0:T(8,128)(2,1)}, u32[]{:S(2)}) copy-start(bf16[256,2048]{1,0:T(8,128)(2,1)} %copy-done.5) | copy-start | bytes 3145732
  467.2 15.3 %collective-permute-start.8 = (f32[256,512]{1,0:T(8,128)}, f32[256,512]{1,0:T(8,128)}, u32[]{:S(2)}, u32[]{:S(2)}) collective-permute-start(f32[256,512]{1,0:T(8,128)} %add.57), channel_id=1, source_target_pairs={{0,4},{1,5},{2,6},{3,7},{4,0},{5,1},{6,2},{7,3},{8,12},{9,13},{10,... | collective-permute-start | bytes 1572872 | tf_op jit(solution)/shard_map/ppermute | solution.py:53
Sparse Core Ops, SparseCore 0:
  12.1 160.3 all-reduce.1
  207.0 100.2 all-gather.2
  341.9 101.0 all-gather.4
